TPU v7x, 32 devices: a whole 2x2x4 slice. The times are simulated.
32 devices in a mesh: tm: 4 (over z), height: 4 (over y, x), width: 2 (over core).
Axes of the slice: x: 2, y: 2, z: 4, core: 2. Of those that a mesh axis runs over, the one named last changes fastest.
Arguments:
- frames: bfloat16 [8, 64, 32, 384], P('tm', 'height', 'width'), may hold values from -20 to 20
- attn_gain: float32 [384], replicated, may hold values from 0.25 to 1.75
- qkv_weight: bfloat16 [384, 1152], replicated, may hold values from -2 to 2
- proj_weight: bfloat16 [384, 384], replicated, may hold values from -0.3125 to 0.3125
- proj_bias: float32 [384], replicated, may hold values from -1.5 to 1.5
- conv_gain: float32 [384], replicated, may hold values from 0.25 to 1.75
- conv_weight: bfloat16 [3, 3, 3, 384, 384], replicated, may hold values from -0.0625 to 0.0625
- conv_bias: float32 [384], replicated, may hold values from -1.5 to 1.5
Outputs:
- decoded: bfloat16 [8, 64, 32, 384], P('tm', 'height', 'width')
All inputs are finite; a program needn't handle non-finite values.
Results may differ from a plain program's by a relative error of at most 0.011.
Values may be sent and summed in bfloat16 or wider, within the bound.
A program may use at most 128 MiB of HBM per device.

v0:
```python
import math

import jax
import jax.numpy as jnp
from jax import lax
from jax.sharding import PartitionSpec as P

epsilon = 1e-06


def shifted(value, axis, by):
    count = lax.axis_size(axis)
    pairs = [(i, i + by) for i in range(count) if 0 <= i + by < count]
    return lax.ppermute(value, axis, pairs)


def with_halo(block, sides, width):
    for axis, dim in sides:
        count = lax.axis_size(axis)
        forward = [(i, i + 1) for i in range(count - 1)]
        backward = [(target, source) for source, target in forward]
        low = lax.ppermute(
            lax.slice_in_dim(block, block.shape[dim] - width, None, axis=dim), axis, forward
        )
        high = lax.ppermute(lax.slice_in_dim(block, 0, width, axis=dim), axis, backward)
        block = jnp.concatenate([low, block, high], axis=dim)
    return block


def rms_scale(values, gain_row):
    widened = values.astype(jnp.float32)
    mean_square = jnp.mean(widened * widened, axis=-1, keepdims=True)
    return widened * lax.rsqrt(mean_square + epsilon) * gain_row


def attend_update(state_now, queries, key_block, value_block, score_scale):
    running_max, running_sum, weighted = state_now
    scores = (
        jnp.einsum("fqc,fnc->fqn", queries, key_block, preferred_element_type=jnp.float32)
        * score_scale
    )
    new_max = jnp.max(scores, axis=-1)
    shrink = jnp.exp(running_max - new_max)
    weights = jnp.exp(scores - new_max[..., None])
    running_sum = running_sum * shrink + jnp.sum(weights, axis=-1)
    summed = jnp.einsum(
        "fqn,fnc->fqc",
        weights.astype(jnp.bfloat16),
        value_block,
        preferred_element_type=jnp.float32,
    )
    weighted = weighted * shrink[..., None] + summed
    return (new_max, running_sum, weighted)


def shards(
    frames, attn_gain, qkv_weight, proj_weight, proj_bias, conv_gain, conv_weight, conv_bias
):
    frame_count, tile_rows, tile_cols, channels = frames.shape
    tile_cells = tile_rows * tile_cols
    flattened = frames.reshape(frame_count, tile_cells, channels)
    attn_in = rms_scale(flattened, attn_gain).astype(jnp.bfloat16)
    score_scale = 1.0 / math.sqrt(channels)
    start_state = (
        jnp.full((frame_count, tile_cells), -jnp.inf, jnp.float32),
        jnp.zeros((frame_count, tile_cells), jnp.float32),
        jnp.zeros((frame_count, tile_cells, channels), jnp.float32),
    )
    queries = jnp.dot(
        attn_in.reshape(-1, channels), qkv_weight[:, :channels], preferred_element_type=jnp.float32
    )
    queries = queries.astype(jnp.bfloat16).reshape(frame_count, tile_cells, channels)
    shard_piece = lax.all_gather(attn_in, ("height", "width"), axis=1, tiled=True)
    piece_cells = shard_piece.shape[1]
    key_value = jnp.dot(
        shard_piece.reshape(-1, channels),
        qkv_weight[:, channels:],
        preferred_element_type=jnp.float32,
    )
    key_value = key_value.astype(jnp.bfloat16).reshape(frame_count, piece_cells, 2 * channels)
    running_max, running_sum, weighted = attend_update(
        start_state, queries, key_value[..., :channels], key_value[..., channels:], score_scale
    )
    attended = (weighted / running_sum[..., None]).astype(jnp.bfloat16)
    projected_out = jnp.dot(
        attended.reshape(-1, channels), proj_weight, preferred_element_type=jnp.float32
    )
    mixed = (
        flattened.reshape(-1, channels).astype(jnp.float32) + projected_out + proj_bias
    ).astype(jnp.bfloat16)
    conv_in = jax.nn.silu(rms_scale(mixed, conv_gain)).astype(jnp.bfloat16)
    conv_in = conv_in.reshape(frame_count, tile_rows, tile_cols, channels)
    earlier = shifted(conv_in, "tm", 1)
    extended = jnp.concatenate([earlier, conv_in], axis=0)
    padded = with_halo(extended, (("height", 1), ("width", 2)), 1)
    windows = [
        padded[
            step_t : step_t + frame_count, step_h : step_h + tile_rows, step_w : step_w + tile_cols
        ]
        for step_t in range(3)
        for step_h in range(3)
        for step_w in range(3)
    ]
    stacked = jnp.concatenate(windows, axis=-1).reshape(frame_count * tile_cells, 27 * channels)
    conv_out = jnp.dot(
        stacked, conv_weight.reshape(27 * channels, channels), preferred_element_type=jnp.float32
    )
    decoded = mixed.astype(jnp.float32) + conv_out + conv_bias
    return decoded.astype(jnp.bfloat16).reshape(frame_count, tile_rows, tile_cols, channels)


def solution(mesh):
    in_specs = (P("tm", "height", "width", None), P(), P(), P(), P(), P(), P(), P())
    out_specs = P("tm", "height", "width", None)
    return jax.shard_map(shards, mesh=mesh, in_specs=in_specs, out_specs=out_specs, check_vma=False)
```

profile of v0, /device:TPU:0, one launch (start us, length us, event | category | flops | bytes accessed | tf_op | source)
XLA Modules:
  0.0 101.1 jit_solution(10051947625321163738)
XLA Ops:
  6.5 0.0 copy-start
  6.5 1.2 %multiply_reduce_fusion.2 = f32[2,16,16]{2,1,0:T(8,128)S(1)} fusion(bf16[2,16,16,384]{3,2,1,0:T(8,128)(2,1)} %param.8), kind=kLoop, calls=%fused_computation.34 | loop fusion | flops 589312 | bytes 395264 | tf_op jit(solution)/shard_map/reduce_sum | solution.py:32
  7.7 0.1 rsqrt.25
  7.8 1.9 %fusion.30 = bf16[2,256,384]{2,1,0:T(8,128)(2,1)} fusion(bf16[2,16,16,384]{3,2,1,0:T(8,128)(2,1)} %param.8, f32[384]{0:T(512)} %param.9, f32[2,256]{1,0:T(2,128)S(1)} %rsqrt.25), kind=kLoop, calls=%fused_computation.28 | loop fusion | flops 786432 | bytes 790016 | tf_op jit(solution)/shard_map/convert_element_type | solution.py:62
  9.7 0.0 all-gather.2.cloned.1.call-update
  9.8 0.1 rsqrt.24
  9.8 1.2 %fusion.32 = bf16[512,384]{1,0:T(8,128)(2,1)S(1)} fusion(bf16[2,16,16,384]{3,2,1,0:T(8,128)(2,1)} %param.8, f32[384]{0:T(512)} %param.9, f32[512]{0:T(512)S(1)} %rsqrt.24), kind=kLoop, calls=%fused_computation.31 | loop fusion | flops 786432 | bytes 790016 | tf_op jit(solution)/shard_map/convert_element_type | solution.py:62
  11.0 1.4 %convolution_convert_fusion.1 = bf16[512,384]{1,0:T(8,128)(2,1)S(1)} fusion(bf16[512,384]{1,0:T(8,128)(2,1)S(1)} %fusion.32, bf16[384,1152]{1,0:T(8,128)(2,1)} %param.10), kind=kOutput, calls=%fused_computation.20 | convolution fusion | flops 151191552 | bytes 1081344 | tf_op jit(solution)/shard_map/dot_general | solution.py:69
  12.4 32.5 %all-gather.2.cloned.1.call-done = bf16[2,2048,384]{2,1,0:T(8,128)(2,1)} async-done(((bf16[2,256,384]{2,1,0:T(8,128)(2,1)}), bf16[2,2048,384]{2,1,0:T(8,128)(2,1)}) %all-gather.2.cloned.1.call-update) | async-done | bytes 3145744 | tf_op jit(solution)/shard_map/all_gather | solution.py:73
  44.8 5.4 %convolution_convert_fusion = bf16[4096,768]{1,0:T(8,128)(2,1)S(1)} fusion(bf16[4096,384]{1,0:T(8,128)(2,1)} %bitcast.93, bf16[384,1152]{1,0:T(8,128)(2,1)} %param.10), kind=kOutput, calls=%fused_computation | convolution fusion | flops 2419064832 | bytes 10027008 | tf_op jit(solution)/shard_map/dot_general | solution.py:75
  50.3 0.0 copy-start.1
  50.3 0.0 copy-start.3
  50.3 1.4 %multiply_reduce_fusion = (f32[2,256]{1,0:T(2,128)S(1)}, f32[2,256,2048]{2,1,0:T(8,128)S(1)}) fusion(bf16[2,256,384]{2,1,0:T(8,128)(2,1)S(1)} %bitcast.79, bf16[2,2048,768]{2,1,0:T(8,128)(2,1)S(1)} %bitcast.80), kind=kOutput, calls=%fused_computation.2 | convolution fusion | flops 807403008 | bytes 7735296 | tf_op jit(solution)/shard_map/fqc,fnc->fqn/dot_general | solution.py:39
  51.7 0.8 fusion
  52.5 1.5 %fusion.24 = bf16[2,256,384]{2,1,0:T(8,128)(2,1)S(1)} fusion(bf16[2,2048,768]{2,1,0:T(8,128)(2,1)S(1)} %bitcast.81, f32[2,256,2048]{2,1,0:T(8,128)S(1)} %get-tuple-element.40, f32[2,256]{1,0:T(2,128)S(1)} %get-tuple-element.39, f32[2,256]{1,0:T(2,128)S(1)} %get-tuple-element.38, f32[2,256]{1,0:T(2,128)S(1)} %get-tuple-element.37), kind=kOutput, calls=%fused_computation.23 | convolution fusion | flops 809041920 | bytes 7739392 | tf_op jit(solution)/shard_map/fqn,fnc->fqc/dot_general | solution.py:46
  54.1 0.5 multiply_reduce_fusion.1
  54.6 0.3 multiply_convert_fusion
  54.9 3.4 %collective-permute-start = (bf16[2,16,16,384]{3,2,1,0:T(8,128)(2,1)S(1)}, bf16[2,16,16,384]{3,2,1,0:T(8,128)(2,1)S(1)}, u32[]{:S(2)}, u32[]{:S(2)}) collective-permute-start(bf16[2,16,16,384]{3,2,1,0:T(8,128)(2,1)S(1)} %bitcast.54), channel_id=1, source_target_pairs={{0,8},{8,16},{16,24},{1,9},{9,17},{17,25},{2,10},{10,18},{18,26},{... | collective-permute-start | bytes 1179656 | tf_op jit(solution)/shard_map/ppermute | solution.py:14
  58.3 8.7 %collective-permute-done = bf16[2,16,16,384]{3,2,1,0:T(8,128)(2,1)S(1)} collective-permute-done((bf16[2,16,16,384]{3,2,1,0:T(8,128)(2,1)S(1)}, bf16[2,16,16,384]{3,2,1,0:T(8,128)(2,1)S(1)}, u32[]{:S(2)}, u32[]{:S(2)}) %collective-permute-start) | collective-permute-done | bytes 393248 | tf_op jit(solution)/shard_map/ppermute | solution.py:14
  67.1 3.4 %collective-permute-start.1 = (bf16[4,1,16,384]{3,2,1,0:T(8,128)(2,1)S(1)}, bf16[4,1,16,384]{3,2,1,0:T(8,128)(2,1)S(1)}, u32[]{:S(2)}, u32[]{:S(2)}) collective-permute-start(bf16[4,1,16,384]{3,2,1,0:T(8,128)(2,1)S(1)} %get-tuple-element.35), channel_id=1, source_target_pairs={{0,2},{2,4},{4,6},{1,3},{3,5},{5,7},{8,10},{10,12},{12,14},{9,11},... | collective-permute-start | bytes 147464 | tf_op jit(solution)/shard_map/ppermute | solution.py:22
  70.4 1.3 %collective-permute-start.2 = (bf16[4,1,16,384]{3,2,1,0:T(8,128)(2,1)S(1)}, bf16[4,1,16,384]{3,2,1,0:T(8,128)(2,1)S(1)}, u32[]{:S(2)}, u32[]{:S(2)}) collective-permute-start(bf16[4,1,16,384]{3,2,1,0:T(8,128)(2,1)S(1)} %get-tuple-element.36), channel_id=1, source_target_pairs={{2,0},{4,2},{6,4},{3,1},{5,3},{7,5},{10,8},{12,10},{14,12},{11,9},... | collective-permute-start | bytes 147464 | tf_op jit(solution)/shard_map/ppermute | solution.py:25
  71.8 0.4 collective-permute-done.1
  72.2 4.3 %collective-permute-done.2 = bf16[4,1,16,384]{3,2,1,0:T(8,128)(2,1)S(1)} collective-permute-done((bf16[4,1,16,384]{3,2,1,0:T(8,128)(2,1)S(1)}, bf16[4,1,16,384]{3,2,1,0:T(8,128)(2,1)S(1)}, u32[]{:S(2)}, u32[]{:S(2)}) %collective-permute-start.2) | collective-permute-done | bytes 49184 | tf_op jit(solution)/shard_map/ppermute | solution.py:25
  76.4 0.2 pad_maximum_fusion.3
  76.6 1.3 %collective-permute-start.4 = (bf16[4,18,1,384]{3,2,1,0:T(2,128)(2,1)S(1)}, bf16[4,18,1,384]{3,2,1,0:T(2,128)(2,1)S(1)}, u32[]{:S(2)}, u32[]{:S(2)}) collective-permute-start(bf16[4,18,1,384]{3,2,1,0:T(2,128)(2,1)S(1)} %get-tuple-element.25), channel_id=1, source_target_pairs={{1,0},{3,2},{5,4},{7,6},{9,8},{11,10},{13,12},{15,14},{17,16},{19,... | collective-permute-start | bytes 165896 | tf_op jit(solution)/shard_map/ppermute | solution.py:25
  77.9 3.2 %collective-permute-start.3 = (bf16[4,18,1,384]{3,2,1,0:T(2,128)(2,1)S(1)}, bf16[4,18,1,384]{3,2,1,0:T(2,128)(2,1)S(1)}, u32[]{:S(2)}, u32[]{:S(2)}) collective-permute-start(bf16[4,18,1,384]{3,2,1,0:T(2,128)(2,1)S(1)} %get-tuple-element.26), channel_id=1, source_target_pairs={{0,1},{2,3},{4,5},{6,7},{8,9},{10,11},{12,13},{14,15},{16,17},{18,... | collective-permute-start | bytes 165896 | tf_op jit(solution)/shard_map/ppermute | solution.py:22
  81.1 0.2 pad_maximum_fusion.1
  81.3 0.3 fusion.39
  81.6 0.0 collective-permute-done.4
  81.6 0.3 collective-permute-done.3
  81.9 1.6 %pad_maximum_fusion = (bf16[4,18,17,384]{3,2,1,0:T(8,128)(2,1)S(1)}, bf16[4,18,17,384]{3,2,1,0:T(8,128)(2,1)S(1)}) fusion(bf16[4,18,1,384]{3,2,1,0:T(2,128)(2,1)S(1)} %collective-permute-done.4, bf16[4,1,16,384]{3,2,1,0:T(8,128)(2,1)S(1)} %collective-permute-done.2, bf16[2,16,16,384]{3,2,1,0:T(8,128)(2,1)S(1)} %bitcast.59, ...), kind=kLoop, calls=%fused_computation.12 | loop fusion | flops 9400320 | bytes 2875392 | tf_op jit(solution)/shard_map/concatenate | solution.py:26
  83.5 0.8 fusion.37
  84.3 0.0 slice-start
  84.3 0.0 copy-start.4
  84.3 0.1 constant_dynamic-update-slice_fusion.25
  84.4 0.1 constant_dynamic-update-slice_fusion.24
  84.4 0.1 constant_dynamic-update-slice_fusion.23
  84.5 0.1 constant_dynamic-update-slice_fusion.22
  84.6 0.1 constant_dynamic-update-slice_fusion.21
  84.7 0.1 constant_dynamic-update-slice_fusion.20
  84.7 0.1 constant_dynamic-update-slice_fusion.19
  84.8 0.1 constant_dynamic-update-slice_fusion.18
  84.9 0.1 constant_dynamic-update-slice_fusion.17
  84.9 0.1 constant_dynamic-update-slice_fusion.16
  85.0 0.1 constant_dynamic-update-slice_fusion.15
  85.1 0.1 constant_dynamic-update-slice_fusion.14
  85.2 0.1 constant_dynamic-update-slice_fusion.13
  85.2 0.0 slice-start.1
  85.2 0.1 constant_dynamic-update-slice_fusion.12
  85.3 0.1 constant_dynamic-update-slice_fusion.11
  85.4 0.1 constant_dynamic-update-slice_fusion.10
  85.5 0.1 constant_dynamic-update-slice_fusion.9
  85.5 0.1 constant_dynamic-update-slice_fusion.8
  85.6 0.1 constant_dynamic-update-slice_fusion.7
  85.7 0.1 constant_dynamic-update-slice_fusion.6
  85.8 0.1 constant_dynamic-update-slice_fusion.5
  85.8 0.3 constant_dynamic-update-slice_fusion.4
  86.2 0.1 constant_dynamic-update-slice_fusion.3
  86.2 0.1 constant_dynamic-update-slice_fusion.2
  86.3 0.1 constant_dynamic-update-slice_fusion.1
  86.4 0.1 constant_dynamic-update-slice_fusion
  86.5 0.0 slice-done
  86.5 1.4 %slice-done.1 = s8[3768320]{0:T(1024)(128)(4,1)S(1)} async-done(((s8[7962624]{0:T(1024)(128)(4,1)}), s8[3768320]{0:T(1024)(128)(4,1)S(1)}, s32[]{:S(2)}) %slice-start.1) | async-done | bytes 3768344
  87.9 6.4 %fusion.18 = bf16[512,384]{1,0:T(8,128)(2,1)} fusion(f32[512,384]{1,0:T(8,128)S(1)} %get-tuple-element.42, bf16[512,10368]{1,0:T(8,128)(2,1)S(1)} %constant_dynamic-update-slice_fusion, bf16[10368,384]{1,0:T(8,128)(2,1)S(1)} %bitcast.92, f32[384]{0:T(512)S(1)} %copy-done.4), kind=kOutput, calls=%fused_computation.21 | convolution fusion | flops 4077453312 | bytes 19760640 | tf_op jit(solution)/shard_map/dot_general | solution.py:105
  (14 shorter events, 0.1 us)
Async XLA Ops:
  6.5 47.5 %copy-start = (bf16[384,384]{1,0:T(8,128)(2,1)S(1)}, bf16[384,384]{1,0:T(8,128)(2,1)}, u32[]{:S(2)}) copy-start(bf16[384,384]{1,0:T(8,128)(2,1)} %param.11) | copy-start | bytes 884740
  6.5 38.3 %all-gather.2.cloned.1.call-start = ((), (), s32[]{:S(2)}) async-start(), calls=%async_computation | async-start | bytes 3538944 | tf_op jit(solution)/shard_map/all_gather | solution.py:73
  50.3 3.8 %copy-start.1 = (bf16[2,16,16,384]{3,2,1,0:T(8,128)(2,1)S(1)}, bf16[2,16,16,384]{3,2,1,0:T(8,128)(2,1)}, u32[]{:S(2)}) copy-start(bf16[2,16,16,384]{3,2,1,0:T(8,128)(2,1)} %param.8) | copy-start | bytes 1179652
  50.3 3.8 %copy-start.3 = (f32[384]{0:T(512)S(1)}, f32[384]{0:T(512)}, u32[]{:S(2)}) copy-start(f32[384]{0:T(512)} %param.12) | copy-start | bytes 4612
  51.7 2.9 %copy-start.2 = (f32[384]{0:T(512)S(1)}, f32[384]{0:T(512)}, u32[]{:S(2)}) copy-start(f32[384]{0:T(512)} %param.13) | copy-start | bytes 4612
  54.9 12.2 %collective-permute-start = (bf16[2,16,16,384]{3,2,1,0:T(8,128)(2,1)S(1)}, bf16[2,16,16,384]{3,2,1,0:T(8,128)(2,1)S(1)}, u32[]{:S(2)}, u32[]{:S(2)}) collective-permute-start(bf16[2,16,16,384]{3,2,1,0:T(8,128)(2,1)S(1)} %bitcast.54), channel_id=1, source_target_pairs={{0,8},{8,16},{16,24},{1,9},{9,17},{17,25},{2,10},{10,18},{18,26},{... | collective-permute-start | bytes 1179656 | tf_op jit(solution)/shard_map/ppermute | solution.py:14
  67.1 5.1 %collective-permute-start.1 = (bf16[4,1,16,384]{3,2,1,0:T(8,128)(2,1)S(1)}, bf16[4,1,16,384]{3,2,1,0:T(8,128)(2,1)S(1)}, u32[]{:S(2)}, u32[]{:S(2)}) collective-permute-start(bf16[4,1,16,384]{3,2,1,0:T(8,128)(2,1)S(1)} %get-tuple-element.35), channel_id=1, source_target_pairs={{0,2},{2,4},{4,6},{1,3},{3,5},{5,7},{8,10},{10,12},{12,14},{9,11},... | collective-permute-start | bytes 147464 | tf_op jit(solution)/shard_map/ppermute | solution.py:22
  70.4 6.0 %collective-permute-start.2 = (bf16[4,1,16,384]{3,2,1,0:T(8,128)(2,1)S(1)}, bf16[4,1,16,384]{3,2,1,0:T(8,128)(2,1)S(1)}, u32[]{:S(2)}, u32[]{:S(2)}) collective-permute-start(bf16[4,1,16,384]{3,2,1,0:T(8,128)(2,1)S(1)} %get-tuple-element.36), channel_id=1, source_target_pairs={{2,0},{4,2},{6,4},{3,1},{5,3},{7,5},{10,8},{12,10},{14,12},{11,9},... | collective-permute-start | bytes 147464 | tf_op jit(solution)/shard_map/ppermute | solution.py:25
  76.6 5.0 %collective-permute-start.4 = (bf16[4,18,1,384]{3,2,1,0:T(2,128)(2,1)S(1)}, bf16[4,18,1,384]{3,2,1,0:T(2,128)(2,1)S(1)}, u32[]{:S(2)}, u32[]{:S(2)}) collective-permute-start(bf16[4,18,1,384]{3,2,1,0:T(2,128)(2,1)S(1)} %get-tuple-element.25), channel_id=1, source_target_pairs={{1,0},{3,2},{5,4},{7,6},{9,8},{11,10},{13,12},{15,14},{17,16},{19,... | collective-permute-start | bytes 165896 | tf_op jit(solution)/shard_map/ppermute | solution.py:25
  77.9 4.0 %collective-permute-start.3 = (bf16[4,18,1,384]{3,2,1,0:T(2,128)(2,1)S(1)}, bf16[4,18,1,384]{3,2,1,0:T(2,128)(2,1)S(1)}, u32[]{:S(2)}, u32[]{:S(2)}) collective-permute-start(bf16[4,18,1,384]{3,2,1,0:T(2,128)(2,1)S(1)} %get-tuple-element.26), channel_id=1, source_target_pairs={{0,1},{2,3},{4,5},{6,7},{8,9},{10,11},{12,13},{14,15},{16,17},{18,... | collective-permute-start | bytes 165896 | tf_op jit(solution)/shard_map/ppermute | solution.py:22
  84.3 2.2 %slice-start = ((s8[7962624]{0:T(1024)(128)(4,1)}), s8[4194304]{0:T(1024)(128)(4,1)S(1)}, s32[]{:S(2)}) async-start(s8[7962624]{0:T(1024)(128)(4,1)} %bitcast.90), calls=%async_computation.1 | async-start | bytes 8388608
  84.3 2.2 %copy-start.4 = (f32[384]{0:T(512)S(1)}, f32[384]{0:T(512)}, u32[]{:S(2)}) copy-start(f32[384]{0:T(512)} %param.15) | copy-start | bytes 4612
  85.2 2.6 %slice-start.1 = ((s8[7962624]{0:T(1024)(128)(4,1)}), s8[3768320]{0:T(1024)(128)(4,1)S(1)}, s32[]{:S(2)}) async-start(s8[7962624]{0:T(1024)(128)(4,1)} %bitcast.90), calls=%async_computation.2 | async-start | bytes 7536640
Sparse Core Ops, SparseCore 0:
  9.9 34.8 all-gather.1
where the time goes:
time: 102 us; the launch traced here: 101 us
  waiting for transfers between devices  46.1 us (45%)
  matrix products  16.6 us (16%)
  between operations  13.8 us (14%)
  starting transfers between devices  12.6 us (12%)
  other arithmetic  7.68 us (8%)
  local copies, waits for them, and re-layouts  4.29 us (4%)
    all_gather x1, waiting for transfers between devices, shards(): lax.all_gather(attn_in, ('height', 'width'), axis=1, tiled=True)  32.5 us
    ppermute x1, waiting for transfers between devices, shifted(): return lax.ppermute(value, axis, pairs)  8.74 us
    ppermute x2, starting transfers between devices, with_halo(): lax.ppermute(lax.slice_in_dim(block, block.shape[dim] - width, None, axis...  6.59 us
    dot_general x1, matrix products, shards(): jnp.dot(stacked, conv_weight.reshape(27 * channels, channels), preferred_...  6.41 us
    dot_general x1, matrix products, shards(): jnp.dot(shard_piece.reshape(-1, channels), qkv_weight[:, channels:], pref...  5.44 us
    ppermute x2, waiting for transfers between devices, with_halo(): lax.ppermute(lax.slice_in_dim(block, 0, width, axis=dim), axis, backward)  4.25 us
    ppermute x1, starting transfers between devices, shifted(): return lax.ppermute(value, axis, pairs)  3.42 us
    convert_element_type x2, other arithmetic, shards(): attn_in = rms_scale(flattened, attn_gain).astype(jnp.bfloat16)  3.07 us
  transfers between devices with their start and end apart: 6, of which 5 were waited for; matrix products, arithmetic and copies ran while one was open for 3% of the time, Pallas kernels for 0%

commit v1 on v0

v1 whole, which is shorter than its diff:
```python
import functools
import math

import jax
import jax.numpy as jnp
from jax import lax
from jax.experimental import pallas as pl
from jax.experimental.pallas import tpu as pltpu
from jax.sharding import PartitionSpec as P

epsilon = 1e-06
MESH = pl.DeviceIdType.MESH
f32 = jnp.float32
bf16 = jnp.bfloat16
lanes = 128

MOVES = [
    (dt, dh, dw)
    for dt in (1, 0)
    for dh in (0, -1, 1)
    for dw in (0, -1, 1)
    if (dt, dh, dw) != (0, 0, 0)
]
CORNERS = {(-1, -1): 0, (-1, 1): 1, (1, -1): 2, (1, 1): 3}


def dot(a, b):
    return jnp.dot(a, b, preferred_element_type=f32)


def dot_t(a, b):
    return lax.dot_general(a, b, (((1,), (1,)), ((), ())), preferred_element_type=f32)


def rms(values, gain_row):
    mean_square = jnp.mean(values * values, axis=-1, keepdims=True)
    return values * lax.rsqrt(mean_square + epsilon) * gain_row


def kernel(
    sizes,
    frames_hbm,
    qkv_hbm,
    proj_hbm,
    convw_hbm,
    attn_gain,
    proj_bias,
    conv_gain,
    conv_bias,
    out_ref,
    frames_v,
    qkv_v,
    proj_v,
    convw_v,
    gathered,
    query,
    value_proj,
    scores,
    weights,
    conv_f32,
    mixed,
    centre,
    columns,
    corners,
    edge,
    shifted,
    total,
    load_sem,
    convw_sem,
    ring_send,
    ring_recv,
    side_send,
    side_recv,
    halo_send,
    halo_recv,
):
    T, H, W, rows, cols, channels = sizes
    cells = rows * cols
    half = cells // 2
    blocks = H * W
    t, h, w = lax.axis_index("tm"), lax.axis_index("height"), lax.axis_index("width")

    loads = [
        pltpu.make_async_copy(frames_hbm, frames_v, load_sem.at[0]),
        pltpu.make_async_copy(qkv_hbm, qkv_v, load_sem.at[1]),
        pltpu.make_async_copy(proj_hbm, proj_v, load_sem.at[2]),
    ]
    for copy in loads:
        copy.start()
    convw_loads = [
        pltpu.make_async_copy(convw_hbm.at[pl.ds(3 * a, 3)], convw_v.at[pl.ds(3 * a, 3)], convw_sem.at[a])
        for a in range(3)
    ]
    for copy in convw_loads:
        copy.start()

    square = H == 4 and W == 2

    def turn(p):
        return p + (p // 2) * (1 - 2 * (p % 2)) if square else p

    pos = turn(h)

    def at_pos(offset):
        return turn((pos + offset + H) % H)

    def device(dt, hh, ww):
        return {"tm": t + dt, "height": hh, "width": ww}

    def inside(dt, dh, dw):
        ok = None
        for value, delta, count in ((t, dt, T), (h, dh, H), (w, dw, W)):
            if delta:
                one = value + delta < count if delta > 0 else value + delta >= 0
                ok = one if ok is None else jnp.logical_and(ok, one)
        return ok

    centre[...] = jnp.zeros_like(centre)
    columns[...] = jnp.zeros_like(columns)
    corners[...] = jnp.zeros_like(corners)

    barrier = pltpu.get_barrier_semaphore()

    def greet(target):
        pl.semaphore_signal(barrier, inc=1, device_id=target, device_id_type=MESH)

    close = 0
    if H > 1:
        greet(device(0, at_pos(1), w))
        greet(device(0, at_pos(-1), w))
        close += 2
    for j in range(1, W):
        greet(device(0, h, (w + j) % W))
        close += 1
    for dt, dh, dw in MOVES:
        @pl.when(inside(-dt, -dh, -dw))
        def _():
            greet(device(-dt, h - dh, w - dw))

    own = h * W + w
    loads[0].wait()
    for f in (1, 0):
        gathered[f, own] = rms(frames_v[f].astype(f32), attn_gain[...]).astype(bf16)

    def count(delta, value, limit):
        one = value + delta < limit if delta > 0 else value + delta >= 0
        return jnp.where(one, 1, 0)

    around = (1 + count(1, h, H) + count(-1, h, H)) * (1 + count(1, w, W) + count(-1, w, W))
    pl.semaphore_wait(barrier, close + around - 1 + count(1, t, T) * around)

    def ring_copy(f, way, step, part):
        sign = 1 if way == 0 else -1
        origin = at_pos(-sign * (step - 1))
        piece = gathered.at[f, origin * W + w, pl.ds(part * half, half)]
        return pltpu.make_async_remote_copy(
            piece,
            piece,
            ring_send.at[f, way, step - 1, part],
            ring_recv.at[f, way, step - 1, part],
            device_id=device(0, at_pos(sign), w),
            device_id_type=MESH,
        )

    def ring_arrival(f, way, step, part):
        sign = 1 if way == 0 else -1
        origin = at_pos(-sign * step)
        piece = gathered.at[f, origin * W + w, pl.ds(part * half, half)]
        return pltpu.make_async_remote_copy(
            piece,
            piece,
            ring_send.at[f, way, step - 1, part],
            ring_recv.at[f, way, step - 1, part],
            device_id=device(0, at_pos(sign), w),
            device_id_type=MESH,
        )

    def parts_of(way, step):
        if 2 * step < H:
            return (0, 1) if way == 0 else (1, 0)
        return (way,)

    def side_copy(f, offset, part, j, incoming=False):
        column = (w - j + W) % W if incoming else w
        piece = gathered.at[f, at_pos(-offset) * W + column, pl.ds(part * half, half)]
        return pltpu.make_async_remote_copy(
            piece,
            piece,
            side_send.at[f, offset, part, j],
            side_recv.at[f, offset, part, j],
            device_id=device(0, h, (w + j) % W),
            device_id_type=MESH,
        )

    def pass_aside(f, offset, part):
        for j in range(1, W):
            side_copy(f, offset, part, j).start()

    steps = H // 2

    def start_own(f):
        if H > 1:
            for k in range(len(parts_of(0, 1))):
                for way in (0, 1):
                    ring_copy(f, way, 1, parts_of(way, 1)[k]).start()
        for part in (0, 1):
            pass_aside(f, 0, part)

    def arrive(f, way, step, k):
        part = parts_of(way, step)[k]
        ring_arrival(f, way, step, part).wait_recv()
        if step < steps and part in parts_of(way, step + 1):
            ring_copy(f, way, step + 1, part).start()
        pass_aside(f, step if way == 0 else H - step, part)

    arrivals = [
        (step, k, way)
        for step in range(1, steps + 1)
        for k in range(len(parts_of(0, step)))
        for way in (0, 1)
    ]

    def finish_gather(f):
        for offset in range(H):
            for part in (0, 1):
                for j in range(1, W):
                    side_copy(f, offset, part, j, incoming=True).wait_recv()

    start_own(1)

    loads[1].wait()
    loads[2].wait()
    value_proj[...] = dot(qkv_v[:, 2 * channels :], proj_v[...]).astype(bf16)
    score_scale = 1.0 / math.sqrt(channels)
    for f in (1, 0):
        q = dot(gathered[f, own], qkv_v[:, :channels]).astype(bf16)
        query[f] = (dot_t(q, qkv_v[:, channels : 2 * channels]) * score_scale).astype(bf16)

    group = math.gcd(blocks, 8)

    def attend(f):
        q = query[f]
        lane_max = None
        for j in range(blocks):
            s = dot_t(q, gathered[f, j])
            scores[:, j * cells : (j + 1) * cells] = s
            for c in range(0, cells, lanes):
                part = s[:, c : c + lanes]
                lane_max = part if lane_max is None else jnp.maximum(lane_max, part)
        row_max = jnp.max(lane_max, axis=-1, keepdims=True)
        lane_sum = None
        summed = None
        for g in range(0, blocks, group):
            for j in range(g, g + group):
                p = jnp.exp(scores[:, j * cells : (j + 1) * cells] - row_max)
                for c in range(0, cells, lanes):
                    part = p[:, c : c + lanes]
                    lane_sum = part if lane_sum is None else lane_sum + part
                weights[:, (j - g) * cells : (j - g + 1) * cells] = p.astype(bf16)
            keys = gathered[f, pl.ds(g, group)].reshape(group * cells, channels)
            one = dot(weights[...], keys)
            summed = one if summed is None else summed + one
        row_sum = jnp.sum(lane_sum, axis=-1, keepdims=True)
        context = (summed / row_sum).astype(bf16)
        projected = dot(context, value_proj[...])
        now = (frames_v[f].astype(f32) + projected + proj_bias[...]).astype(bf16)
        mixed[f] = now
        v = rms(now.astype(f32), conv_gain[...])
        c_in = v / (1.0 + jnp.exp(-v))
        centre[2 + f, pl.ds(cols, cells)] = c_in.astype(bf16)
        for c in range(channels // lanes):
            span = slice(c * lanes, (c + 1) * lanes)
            conv_f32[c] = c_in[:, span]
            edge[f, 0, :, span] = conv_f32[c, pl.ds(0, rows, cols), :].astype(bf16)
            edge[f, 1, :, span] = conv_f32[c, pl.ds(cols - 1, rows, cols), :].astype(bf16)

    def halo_copy(f, index):
        dt, dh, dw = MOVES[index]
        slot = f if dt else 2 + f
        row = {0: cols, -1: cols, 1: rows * cols}[dh]
        if dh == 0 and dw == 0:
            src = centre.at[2 + f, pl.ds(cols, cells)]
            dst = centre.at[slot, pl.ds(cols, cells)]
        elif dw == 0:
            src = centre.at[2 + f, pl.ds(row, cols)]
            dst = centre.at[slot, pl.ds((rows + 1) * cols if dh < 0 else 0, cols)]
        elif dh == 0:
            src = edge.at[f, 0 if dw < 0 else 1]
            dst = columns.at[slot, 1 if dw < 0 else 0]
        else:
            src = centre.at[2 + f, pl.ds(row, cols)]
            dst = corners.at[slot, CORNERS[(-dh, -dw)]]
        return pltpu.make_async_remote_copy(
            src,
            dst,
            halo_send.at[f, index],
            halo_recv.at[f, index],
            device_id=device(dt, h + dh, w + dw),
            device_id_type=MESH,
        )

    def send_halos(f):
        for index, move in enumerate(MOVES):
            @pl.when(inside(*move))
            def _():
                halo_copy(f, index).start()

    def wait_halos(f, ahead):
        for index, (dt, dh, dw) in enumerate(MOVES):
            if dt == ahead:
                @pl.when(inside(-dt, -dh, -dw))
                def _():
                    halo_copy(f, index).wait_recv()

    def shift(s):
        place = lax.broadcasted_iota(jnp.int32, (cols, channels), 0)
        first, last = place == 0, place == cols - 1
        low, high = columns[s, 0].astype(f32), columns[s, 1].astype(f32)
        for r in range(rows + 2):
            here = centre[s, r * cols : (r + 1) * cols]
            x = here.astype(f32)
            if 0 < r <= rows:
                before, after = low[r - 1 : r], high[r - 1 : r]
            else:
                c = 0 if r == 0 else 2
                before = corners[s, c].astype(f32)[cols - 1 : cols]
                after = corners[s, c + 1].astype(f32)[0:1]
            there = pl.ds(r * cols, cols)
            shifted[s, there, 0:channels] = jnp.where(
                first, before, pltpu.roll(x, 1, axis=0)
            ).astype(bf16)
            shifted[s, there, channels : 2 * channels] = here
            shifted[s, there, 2 * channels : 3 * channels] = jnp.where(
                last, after, pltpu.roll(x, cols - 1, axis=0)
            ).astype(bf16)

    def conv(o, a):
        s = o + a
        value = None
        for b in range(3):
            one = dot(shifted[s, b * cols : b * cols + cells], convw_v[3 * a + b])
            value = one if value is None else value + one
        return value

    early = 2 if steps > 1 else 0
    for step, k, way in arrivals[:early]:
        arrive(1, way, step, k)
    start_own(0)
    for step, k, way in arrivals[early:]:
        arrive(1, way, step, k)
    finish_gather(1)
    for step, k, way in arrivals[:early]:
        arrive(0, way, step, k)
    attend(1)
    send_halos(1)
    for copy in convw_loads:
        copy.wait()
    for step, k, way in arrivals[early : 2 * early]:
        arrive(0, way, step, k)
    wait_halos(1, 0)
    shift(3)
    total[1] = conv(1, 2)
    for step, k, way in arrivals[2 * early :]:
        arrive(0, way, step, k)
    finish_gather(0)
    attend(0)
    send_halos(0)
    wait_halos(0, 0)
    shift(2)
    total[0] = conv(0, 2)
    total[1] += conv(1, 1)
    wait_halos(1, 1)
    shift(1)
    total[0] += conv(0, 1)
    total[1] += conv(1, 0)
    out_ref[1] = (mixed[1].astype(f32) + total[1] + conv_bias[...]).astype(bf16)
    wait_halos(0, 1)
    shift(0)
    out_ref[0] = (
        mixed[0].astype(f32) + (total[0] + conv(0, 0)) + conv_bias[...]
    ).astype(bf16)

    for f in (1, 0):
        for step in range(1, steps + 1):
            for way in (0, 1):
                for part in parts_of(way, step):
                    ring_copy(f, way, step, part).wait_send()
        for offset in range(H):
            for part in (0, 1):
                for j in range(1, W):
                    side_copy(f, offset, part, j).wait_send()
        for index, move in enumerate(MOVES):
            @pl.when(inside(*move))
            def _():
                halo_copy(f, index).wait_send()


def shards(
    mesh_sizes,
    frames,
    attn_gain,
    qkv_weight,
    proj_weight,
    proj_bias,
    conv_gain,
    conv_weight,
    conv_bias,
):
    T, H, W = mesh_sizes
    frame_count, rows, cols, channels = frames.shape
    cells = rows * cols
    blocks = H * W
    group = math.gcd(blocks, 8)
    anywhere = pl.BlockSpec(memory_space=pl.ANY)
    vmem = pl.BlockSpec(memory_space=pltpu.VMEM)
    dma = pltpu.SemaphoreType.DMA
    steps = max(H // 2, 1)
    decoded = pl.pallas_call(
        functools.partial(kernel, (T, H, W, rows, cols, channels)),
        out_shape=jax.ShapeDtypeStruct((frame_count, cells, channels), bf16),
        in_specs=[anywhere] * 4 + [vmem] * 4,
        out_specs=vmem,
        scratch_shapes=[
            pltpu.VMEM((2, cells, channels), bf16),
            pltpu.VMEM((channels, 3 * channels), bf16),
            pltpu.VMEM((channels, channels), bf16),
            pltpu.VMEM((9, 3 * channels, channels), bf16),
            pltpu.VMEM((2, blocks, cells, channels), bf16),
            pltpu.VMEM((2, cells, channels), bf16),
            pltpu.VMEM((channels, channels), bf16),
            pltpu.VMEM((cells, blocks * cells), f32),
            pltpu.VMEM((cells, group * cells), bf16),
            pltpu.VMEM((channels // lanes, cells, lanes), f32),
            pltpu.VMEM((2, cells, channels), bf16),
            pltpu.VMEM((4, (rows + 2) * cols, channels), bf16),
            pltpu.VMEM((4, 2, rows, channels), bf16),
            pltpu.VMEM((4, 4, cols, channels), bf16),
            pltpu.VMEM((2, 2, rows, channels), bf16),
            pltpu.VMEM((4, (rows + 2) * cols, 3 * channels), bf16),
            pltpu.VMEM((2, cells, channels), f32),
            dma((3,)),
            dma((3,)),
            dma((2, 2, steps, 2)),
            dma((2, 2, steps, 2)),
            dma((2, H, 2, W)),
            dma((2, H, 2, W)),
            dma((2, len(MOVES))),
            dma((2, len(MOVES))),
        ],
        compiler_params=pltpu.CompilerParams(
            collective_id=0, has_side_effects=True, vmem_limit_bytes=60 * 2**20
        ),
    )(
        frames.reshape(frame_count, cells, channels),
        qkv_weight,
        proj_weight,
        conv_weight.reshape(9, 3 * channels, channels),
        attn_gain.reshape(1, channels),
        proj_bias.reshape(1, channels),
        conv_gain.reshape(1, channels),
        conv_bias.reshape(1, channels),
    )
    return decoded.reshape(frame_count, rows, cols, channels)


def solution(mesh):
    sizes = tuple(mesh.shape[axis] for axis in ("tm", "height", "width"))
    in_specs = (P("tm", "height", "width", None), P(), P(), P(), P(), P(), P(), P())
    out_specs = P("tm", "height", "width", None)
    return jax.shard_map(
        functools.partial(shards, sizes),
        mesh=mesh,
        in_specs=in_specs,
        out_specs=out_specs,
        check_vma=False,
    )
```

time: 102 us -> 43.4 us (0.43)
  waiting for transfers between devices: 46.1 us -> 0 us
  Pallas kernels: 0 us -> 36.3 us
  matrix products: 16.6 us -> 0 us
  between operations: 13.8 us -> 0.01 us
  starting transfers between devices: 12.6 us -> 0 us
  other arithmetic: 7.68 us -> 0 us
  local copies, waits for them, and re-layouts: 4.29 us -> 6.8 us
    pallas_call x0 -> x1, Pallas kernels: none -> 36.3 us  [shards(): pl.pallas_call(functools.partial(kernel, (T, H, W, rows, cols, channels))...]
    all_gather x1 -> x0, waiting for transfers between devices: 32.5 us -> none  [shards(): lax.all_gather(attn_in, ('height', 'width'), axis=1, tiled=True)]
    dot_general x6 -> x0, matrix products: 16.6 us -> none  [the longest x1 6.41 us: shards(): jnp.dot(stacked, conv_weight.reshape(27 * channels, channels), preferred_...]
    ppermute x5 -> x0, waiting for transfers between devices: 13.7 us -> none  [the longest x1 8.74 us: shifted(): return lax.ppermute(value, axis, pairs)]
    ppermute x5 -> x0, starting transfers between devices: 12.6 us -> none  [the longest x2 6.59 us: with_halo(): lax.ppermute(lax.slice_in_dim(block, block.shape[dim] - width, None, axis...]
    reshape x0 -> x4, local copies, waits for them, and re-layouts: none -> 5.02 us  [the longest x1 1.27 us: shards(): conv_bias.reshape(1, channels)]
    convert_element_type x3 -> x0, other arithmetic: 3.36 us -> none  [the longest x2 3.07 us: shards(): attn_in = rms_scale(flattened, attn_gain).astype(jnp.bfloat16)]
    reduce_sum x2 -> x0, other arithmetic: 2 us -> none  [the longest x1 1.19 us: rms_scale(): mean_square = jnp.mean(widened * widened, axis=-1, keepdims=True)]
  transfers between devices with their start and end apart: 6 -> 0, of which waited for: 5 -> 0; matrix products, arithmetic and copies ran while one was open for 3% -> 0% of each run, Pallas kernels for 0% -> 0%
where the time goes in v1:
time: 43.4 us; the launch traced here: 43.2 us
  Pallas kernels  36.3 us (84%)
  local copies, waits for them, and re-layouts  6.8 us (16%)
    pallas_call x1, Pallas kernels, shards(): pl.pallas_call(functools.partial(kernel, (T, H, W, rows, cols, channels))...  36.3 us
    unnamed x1, local copies, waits for them, and re-layouts  1.78 us
    reshape x1, local copies, waits for them, and re-layouts, shards(): conv_bias.reshape(1, channels)  1.27 us
    reshape x1, local copies, waits for them, and re-layouts, shards(): proj_bias.reshape(1, channels)  1.26 us
    reshape x1, local copies, waits for them, and re-layouts, shards(): attn_gain.reshape(1, channels)  1.24 us
    reshape x1, local copies, waits for them, and re-layouts, shards(): conv_gain.reshape(1, channels)  1.24 us

profile of v1, /device:TPU:0, one launch (start us, length us, event | category | flops | bytes accessed | tf_op | source)
XLA Modules:
  0.0 43.2 jit_solution(8228068309141834906)
XLA Ops:
  0.0 1.2 %reshape.23.attn_gain = f32[1,384]{1,0:T(1,128)} reshape(f32[384]{0:T(512)} %param.9) | data formatting | bytes 3072 | tf_op jit(solution)/shard_map/reshape | solution.py:458
  1.2 1.3 %reshape.24.proj_bias = f32[1,384]{1,0:T(1,128)} reshape(f32[384]{0:T(512)} %param.12) | data formatting | bytes 3072 | tf_op jit(solution)/shard_map/reshape | solution.py:459
  2.5 1.2 %reshape.25.conv_gain = f32[1,384]{1,0:T(1,128)} reshape(f32[384]{0:T(512)} %param.13) | data formatting | bytes 3072 | tf_op jit(solution)/shard_map/reshape | solution.py:460
  3.7 1.3 %reshape.26.conv_bias = f32[1,384]{1,0:T(1,128)} reshape(f32[384]{0:T(512)} %param.15) | data formatting | bytes 3072 | tf_op jit(solution)/shard_map/reshape | solution.py:461
  5.0 36.3 %shard_map.82 = bf16[2,256,384]{2,1,0:T(8,128)(2,1)} custom-call(bf16[2,256,384]{2,1,0:T(8,128)(2,1)} %bitcast.5, bf16[384,1152]{1,0:T(8,128)(2,1)} %qkv_hbm.1, bf16[384,384]{1,0:T(8,128)(2,1)} %proj_hbm.1, bf16[9,1152,384]{2,1,0:T(8,128)(2,1)} %bitcast.3, f32[1,384]{1,0:T(1,128)} %reshape.23.attn_gain, f32[1,384]{1,0:T(1,128)} %reshape.24.proj_bias, ...), custom_call_target="tpu_custom_call" | custom-call | tf_op jit(solution)/shard_map/pallas_call | solution.py:418
  41.4 1.8 %copy.10 = bf16[2,16,16,384]{3,2,1,0:T(8,128)(2,1)} copy(bf16[2,16,16,384]{3,2,1,0:T(8,128)(2,1)} %bitcast.4) | data formatting | bytes 786432

commit v2 on v1

--- a/solution.py
+++ b/solution.py
@@ -32,6 +32,10 @@
     return lax.dot_general(a, b, (((1,), (1,)), ((), ())), preferred_element_type=f32)
 
 
+def row(vector):
+    return vector[...].reshape(1, vector.shape[0])
+
+
 def rms(values, gain_row):
     mean_square = jnp.mean(values * values, axis=-1, keepdims=True)
     return values * lax.rsqrt(mean_square + epsilon) * gain_row
@@ -43,11 +47,16 @@
     qkv_hbm,
     proj_hbm,
     convw_hbm,
+    attn_gain_hbm,
+    proj_bias_hbm,
+    conv_gain_hbm,
+    conv_bias_hbm,
+    out_hbm,
     attn_gain,
     proj_bias,
     conv_gain,
     conv_bias,
-    out_ref,
+    out_v,
     frames_v,
     qkv_v,
     proj_v,
@@ -66,6 +75,7 @@
     shifted,
     total,
     load_sem,
+    out_sem,
     convw_sem,
     ring_send,
     ring_recv,
@@ -82,8 +92,12 @@
 
     loads = [
         pltpu.make_async_copy(frames_hbm, frames_v, load_sem.at[0]),
-        pltpu.make_async_copy(qkv_hbm, qkv_v, load_sem.at[1]),
-        pltpu.make_async_copy(proj_hbm, proj_v, load_sem.at[2]),
+        pltpu.make_async_copy(attn_gain_hbm, attn_gain, load_sem.at[1]),
+        pltpu.make_async_copy(qkv_hbm, qkv_v, load_sem.at[2]),
+        pltpu.make_async_copy(proj_hbm, proj_v, load_sem.at[3]),
+        pltpu.make_async_copy(proj_bias_hbm, proj_bias, load_sem.at[4]),
+        pltpu.make_async_copy(conv_gain_hbm, conv_gain, load_sem.at[5]),
+        pltpu.make_async_copy(conv_bias_hbm, conv_bias, load_sem.at[6]),
     ]
     for copy in loads:
         copy.start()
@@ -91,8 +105,6 @@
         pltpu.make_async_copy(convw_hbm.at[pl.ds(3 * a, 3)], convw_v.at[pl.ds(3 * a, 3)], convw_sem.at[a])
         for a in range(3)
     ]
-    for copy in convw_loads:
-        copy.start()
 
     square = H == 4 and W == 2
 
@@ -139,8 +151,9 @@
 
     own = h * W + w
     loads[0].wait()
+    loads[1].wait()
     for f in (1, 0):
-        gathered[f, own] = rms(frames_v[f].astype(f32), attn_gain[...]).astype(bf16)
+        gathered[f, own] = rms(frames_v[f].astype(f32), row(attn_gain)).astype(bf16)
 
     def count(delta, value, limit):
         one = value + delta < limit if delta > 0 else value + delta >= 0
@@ -227,9 +240,11 @@
                     side_copy(f, offset, part, j, incoming=True).wait_recv()
 
     start_own(1)
-
-    loads[1].wait()
-    loads[2].wait()
+    for copy in convw_loads:
+        copy.start()
+
+    for copy in loads[2:]:
+        copy.wait()
     value_proj[...] = dot(qkv_v[:, 2 * channels :], proj_v[...]).astype(bf16)
     score_scale = 1.0 / math.sqrt(channels)
     for f in (1, 0):
@@ -263,9 +278,9 @@
         row_sum = jnp.sum(lane_sum, axis=-1, keepdims=True)
         context = (summed / row_sum).astype(bf16)
         projected = dot(context, value_proj[...])
-        now = (frames_v[f].astype(f32) + projected + proj_bias[...]).astype(bf16)
+        now = (frames_v[f].astype(f32) + projected + row(proj_bias)).astype(bf16)
         mixed[f] = now
-        v = rms(now.astype(f32), conv_gain[...])
+        v = rms(now.astype(f32), row(conv_gain))
         c_in = v / (1.0 + jnp.exp(-v))
         centre[2 + f, pl.ds(cols, cells)] = c_in.astype(bf16)
         for c in range(channels // lanes):
@@ -341,6 +356,9 @@
             one = dot(shifted[s, b * cols : b * cols + cells], convw_v[3 * a + b])
             value = one if value is None else value + one
         return value
+
+    def out_copy(f):
+        return pltpu.make_async_copy(out_v.at[f], out_hbm.at[f], out_sem.at[f])
 
     early = 2 if steps > 1 else 0
     for step, k, way in arrivals[:early]:
@@ -373,13 +391,18 @@
     shift(1)
     total[0] += conv(0, 1)
     total[1] += conv(1, 0)
-    out_ref[1] = (mixed[1].astype(f32) + total[1] + conv_bias[...]).astype(bf16)
+    out_v[1] = (mixed[1].astype(f32) + total[1] + row(conv_bias)).astype(bf16)
+    out_copy(1).start()
     wait_halos(0, 1)
     shift(0)
-    out_ref[0] = (
-        mixed[0].astype(f32) + (total[0] + conv(0, 0)) + conv_bias[...]
+    out_v[0] = (
+        mixed[0].astype(f32) + (total[0] + conv(0, 0)) + row(conv_bias)
     ).astype(bf16)
 
+    out_copy(0).start()
+
+    for f in (1, 0):
+        out_copy(f).wait()
     for f in (1, 0):
         for step in range(1, steps + 1):
             for way in (0, 1):
@@ -412,15 +435,20 @@
     blocks = H * W
     group = math.gcd(blocks, 8)
     anywhere = pl.BlockSpec(memory_space=pl.ANY)
-    vmem = pl.BlockSpec(memory_space=pltpu.VMEM)
     dma = pltpu.SemaphoreType.DMA
     steps = max(H // 2, 1)
+    limit = 60 << 20
     decoded = pl.pallas_call(
         functools.partial(kernel, (T, H, W, rows, cols, channels)),
         out_shape=jax.ShapeDtypeStruct((frame_count, cells, channels), bf16),
-        in_specs=[anywhere] * 4 + [vmem] * 4,
-        out_specs=vmem,
+        in_specs=[pl.BlockSpec(memory_space=pltpu.HBM)] * 8,
+        out_specs=anywhere,
         scratch_shapes=[
+            pltpu.VMEM((channels,), f32),
+            pltpu.VMEM((channels,), f32),
+            pltpu.VMEM((channels,), f32),
+            pltpu.VMEM((channels,), f32),
+            pltpu.VMEM((2, cells, channels), bf16),
             pltpu.VMEM((2, cells, channels), bf16),
             pltpu.VMEM((channels, 3 * channels), bf16),
             pltpu.VMEM((channels, channels), bf16),
@@ -438,7 +466,8 @@
             pltpu.VMEM((2, 2, rows, channels), bf16),
             pltpu.VMEM((4, (rows + 2) * cols, 3 * channels), bf16),
             pltpu.VMEM((2, cells, channels), f32),
-            dma((3,)),
+            dma((7,)),
+            dma((2,)),
             dma((3,)),
             dma((2, 2, steps, 2)),
             dma((2, 2, steps, 2)),
@@ -448,17 +477,17 @@
             dma((2, len(MOVES))),
         ],
         compiler_params=pltpu.CompilerParams(
-            collective_id=0, has_side_effects=True, vmem_limit_bytes=60 * 2**20
+            collective_id=0, has_side_effects=True, vmem_limit_bytes=limit
         ),
     )(
         frames.reshape(frame_count, cells, channels),
         qkv_weight,
         proj_weight,
         conv_weight.reshape(9, 3 * channels, channels),
-        attn_gain.reshape(1, channels),
-        proj_bias.reshape(1, channels),
-        conv_gain.reshape(1, channels),
-        conv_bias.reshape(1, channels),
+        attn_gain,
+        proj_bias,
+        conv_gain,
+        conv_bias,
     )
     return decoded.reshape(frame_count, rows, cols, channels)
 

time: 43.4 us -> 37.6 us (0.87)
  local copies, waits for them, and re-layouts: 6.8 us -> 1.78 us
  Pallas kernels: 36.3 us -> 35.6 us
    reshape x4 -> x0, local copies, waits for them, and re-layouts: 5.02 us -> none  [the longest x1 1.27 us: shards(): conv_bias.reshape(1, channels)]
    pallas_call x1, Pallas kernels: 36.3 us -> 35.6 us  [shards(): pl.pallas_call(functools.partial(kernel, (T, H, W, rows, cols, channels))...]
where the time goes in v2:
time: 37.6 us; the launch traced here: 37.4 us
  Pallas kernels  35.6 us (95%)
  local copies, waits for them, and re-layouts  1.78 us (5%)
    pallas_call x1, Pallas kernels, shards(): pl.pallas_call(functools.partial(kernel, (T, H, W, rows, cols, channels))...  35.6 us
    unnamed x1, local copies, waits for them, and re-layouts  1.78 us

profile of v2, /device:TPU:0, one launch (start us, length us, event | category | flops | bytes accessed | tf_op | source)
XLA Modules:
  0.0 37.4 jit_solution(8143221211852553926)
XLA Ops:
  0.0 35.6 %shard_map.82 = bf16[2,256,384]{2,1,0:T(8,128)(2,1)} custom-call(bf16[2,256,384]{2,1,0:T(8,128)(2,1)} %bitcast.5, bf16[384,1152]{1,0:T(8,128)(2,1)} %qkv_hbm.1, bf16[384,384]{1,0:T(8,128)(2,1)} %proj_hbm.1, bf16[9,1152,384]{2,1,0:T(8,128)(2,1)} %bitcast.3, f32[384]{0:T(512)} %attn_gain_hbm.1, f32[384]{0:T(512)} %proj_bias_hbm.1, f32[384]{0:T(512)} %conv_gain_hbm.1, ...), custom_call_target="tpu_custom_call" | custom-call | tf_op jit(solution)/shard_map/pallas_call | solution.py:441
  35.6 1.8 %copy.10 = bf16[2,16,16,384]{3,2,1,0:T(8,128)(2,1)} copy(bf16[2,16,16,384]{3,2,1,0:T(8,128)(2,1)} %bitcast.4) | data formatting | bytes 786432

commit v3 on v2

--- a/solution.py
+++ b/solution.py
@@ -17,8 +17,8 @@
 MOVES = [
     (dt, dh, dw)
     for dt in (1, 0)
-    for dh in (0, -1, 1)
-    for dw in (0, -1, 1)
+    for dh in (-1, 1, 0)
+    for dw in (-1, 1, 0)
     if (dt, dh, dw) != (0, 0, 0)
 ]
 CORNERS = {(-1, -1): 0, (-1, 1): 1, (1, -1): 2, (1, 1): 3}

time: 37.6 us -> 38.3 us (1.019)
  the two profiles are of different devices: /device:TPU:0 before, /device:TPU:21 now
where the time goes in v3:
time: 38.3 us; the launch traced here: 38.2 us
  Pallas kernels  36.4 us (95%)
  local copies, waits for them, and re-layouts  1.78 us (5%)
    pallas_call x1, Pallas kernels, shards(): pl.pallas_call(functools.partial(kernel, (T, H, W, rows, cols, channels))...  36.4 us
    unnamed x1, local copies, waits for them, and re-layouts  1.78 us

profile of v3, /device:TPU:21, one launch (start us, length us, event | category | flops | bytes accessed | tf_op | source)
XLA Modules:
  0.0 38.2 jit_solution(6318146665414620750)
XLA Ops:
  0.0 36.4 %shard_map.82 = bf16[2,256,384]{2,1,0:T(8,128)(2,1)} custom-call(bf16[2,256,384]{2,1,0:T(8,128)(2,1)} %bitcast.5, bf16[384,1152]{1,0:T(8,128)(2,1)} %qkv_hbm.1, bf16[384,384]{1,0:T(8,128)(2,1)} %proj_hbm.1, bf16[9,1152,384]{2,1,0:T(8,128)(2,1)} %bitcast.3, f32[384]{0:T(512)} %attn_gain_hbm.1, f32[384]{0:T(512)} %proj_bias_hbm.1, f32[384]{0:T(512)} %conv_gain_hbm.1, ...), custom_call_target="tpu_custom_call" | custom-call | tf_op jit(solution)/shard_map/pallas_call | solution.py:441
  36.4 1.8 %copy.10 = bf16[2,16,16,384]{3,2,1,0:T(8,128)(2,1)} copy(bf16[2,16,16,384]{3,2,1,0:T(8,128)(2,1)} %bitcast.4) | data formatting | bytes 786432
